TPU v7x, 256 devices: a whole 4x4x8 slice. The times are simulated.
256 devices in a mesh: row: 8 (over y, core), col: 32 (over z, x).
Axes of the slice: x: 4, y: 4, z: 8, core: 2. Of those that a mesh axis runs over, the one named last changes fastest.
Arguments:
- ancestor: bfloat16 [16384, 16384], P('row', 'col'), may hold values from -6 to 6, as said below
- panels: bfloat16 [3, 512, 16384], P(None, 'col', 'row'), may hold values from -0.0625 to 0.0625
- diag_inverse: float32 [3, 512, 512], replicated, may hold values from -6 to 6, as said below
- supernode_blocks: int32 [3, 4], replicated, may hold values from 0 to 127, as said below
- row_lists: int32 [3, 64], replicated, may hold values from 0 to 127, as said below
Outputs:
- updated: bfloat16 [16384, 16384], P('row', 'col')
Inputs may be any that keep to these rules, and one draw needn't show every extreme that they name: ancestor is exactly symmetric. `diag_inverse`: each supernode's block is exactly symmetric. `supernode_blocks`: the 3 times 512 / 128 block numbers are all distinct. `row_lists`: each row holds 64 distinct block numbers; row s holds every block of the supernodes before s and none of supernode s or of later ones.
All inputs are finite; a program needn't handle non-finite values.
Results may differ from a plain program's by a relative error of at most 0.002.
Values may be sent and summed in bfloat16 or wider, within the bound.
No kernel may reach another device: no remote copies, remote signals or barrier semaphores. Data moves between devices by JAX's collectives and lax.ppermute only.
A program may use at most 64 MiB of HBM per device.

v0:
```python
import jax
import jax.numpy as jnp
from jax import lax
from jax.sharding import PartitionSpec as P

W = 512
B = 128
S = 3


def spread(value, axis, source):
    kept = jnp.where(lax.axis_index(axis) == source, value, 0).astype(value.dtype)
    return lax.psum(kept, axis)


def block_flags(listed, first_block, block_count):
    block_ids = first_block + jnp.arange(block_count, dtype=jnp.int32)
    return jnp.any(block_ids[:, None] == listed[None, :], axis=1)


def local(ancestor, panels, diag_inverse, supernode_blocks, row_lists):
    row_count = lax.axis_size("row")
    col_count = lax.axis_size("col")
    row_pos = lax.axis_index("row")
    col_pos = lax.axis_index("col")
    local_rows, local_cols = ancestor.shape
    per_node = W // B
    row_blocks = local_rows // B
    col_blocks = local_cols // B
    col_ratio = col_count // row_count
    first_rowblock = row_pos * row_blocks
    first_colblock = col_pos * col_blocks
    current = ancestor
    for supernode in range(S):
        listed = row_lists[supernode]
        owned_blocks = supernode_blocks[supernode]
        row_flags = block_flags(listed, first_rowblock, row_blocks)
        col_flags = block_flags(listed, first_colblock, col_blocks)
        panel_rows = lax.all_gather(panels[supernode], "col", axis=0, tiled=True)
        panel_rows = jnp.where(
            row_flags[None, :, None], panel_rows.reshape(W, row_blocks, B), 0
        ).reshape(W, local_rows)
        partial_value = -lax.dot_general(
            current, panel_rows, (((0,), (1,)), ((), ())), preferred_element_type=jnp.float32
        )
        col_sum = lax.psum(partial_value, "row")
        col_update = (
            jnp.where(col_flags[:, None, None], col_sum.reshape(col_blocks, B, W), 0.0)
            .reshape(local_cols, W)
            .astype(jnp.bfloat16)
        )
        slab_list = [
            spread(col_update, "col", col_ratio * row_pos + shift_idx)
            for shift_idx in range(col_ratio)
        ]
        row_update = jnp.concatenate(slab_list, axis=0)
        cross_part = jnp.dot(panel_rows, row_update, preferred_element_type=jnp.float32)
        cross_term = lax.psum(cross_part.astype(jnp.bfloat16), "row").astype(jnp.float32)
        diag_block = (diag_inverse[supernode] - 0.5 * (cross_term + cross_term.T)).astype(
            jnp.bfloat16
        )
        col_match = (first_colblock + jnp.arange(col_blocks, dtype=jnp.int32))[
            :, None
        ] == owned_blocks[None, :]
        row_match = (first_rowblock + jnp.arange(row_blocks, dtype=jnp.int32))[
            :, None
        ] == owned_blocks[None, :]
        col_hit = jnp.any(col_match, axis=1)
        row_hit = jnp.any(row_match, axis=1)
        col_select = col_match.astype(jnp.bfloat16)
        row_select = row_match.astype(jnp.bfloat16)
        column_fill = jnp.einsum(
            "rkb,jk->rjb",
            row_update.reshape(local_rows, per_node, B),
            col_select,
            preferred_element_type=jnp.float32,
        ).astype(jnp.bfloat16)
        blocks_view = jnp.where(
            col_hit[None, :, None], column_fill, current.reshape(local_rows, col_blocks, B)
        )
        row_fill = jnp.einsum(
            "jkb,ik->ibj",
            col_update.reshape(local_cols, per_node, B),
            row_select,
            preferred_element_type=jnp.float32,
        ).astype(jnp.bfloat16)
        rows_view = jnp.where(
            row_hit[:, None, None], row_fill, blocks_view.reshape(row_blocks, B, local_cols)
        )
        corner = jnp.einsum(
            "ik,kalb,jl->iajb",
            row_select,
            diag_block.reshape(per_node, B, per_node, B),
            col_select,
            preferred_element_type=jnp.float32,
        ).astype(jnp.bfloat16)
        corner_hit = row_hit[:, None, None, None] & col_hit[None, None, :, None]
        grid_view = jnp.where(corner_hit, corner, rows_view.reshape(row_blocks, B, col_blocks, B))
        current = grid_view.reshape(local_rows, local_cols)
    return current


def solution(mesh):
    in_specs = (P("row", "col"), P(None, "col", "row"), P(), P(), P())
    out_specs = P("row", "col")
    return jax.shard_map(local, mesh=mesh, in_specs=in_specs, out_specs=out_specs, check_vma=False)
```

profile of v0, /device:TPU:2, one launch (start us, length us, event | category | flops | bytes accessed | tf_op | source)
XLA Modules:
  0.0 1100.6 jit_solution(17126207968095562700)
XLA Ops:
  9.6 79.9 %all-gather.11.cloned.1.call-done = bf16[1,512,2048]{2,1,0:T(8,128)(2,1)} async-done(((bf16[1,16,2048]{2,1,0:T(8,128)(2,1)}), bf16[1,512,2048]{2,1,0:T(8,128)(2,1)}) %all-gather.11.cloned.1.call-update) | async-done | bytes 2097168 | tf_op jit(solution)/shard_map/all_gather | solution.py:39
  93.0 50.2 %all-reduce.24 = bf16[512,512]{0,1:T(8,128)(2,1)S(1)} all-reduce(f32[512,512]{0,1:T(8,128)S(1)} %fusion.11), channel_id=1, replica_groups=mesh['row'=8,'col'=32] {'row'}, use_global_device_ids=true, to_apply=%region_12.13 | all-reduce | flops 262144 | bytes 1572864 | tf_op jit(solution)/shard_map/psum | solution.py:46
  145.5 152.2 %all-reduce.23.cloned.1.call-done = (bf16[512,512]{0,1:T(8,128)(2,1)}, bf16[512,512]{0,1:T(8,128)(2,1)}, bf16[512,512]{0,1:T(8,128)(2,1)}, bf16[512,512]{0,1:T(8,128)(2,1)}) async-done(((bf16[512,512]{0,1:T(8,128)(2,1)}, bf16[512,512]{0,1:T(8,128)(2,1)}, bf16[512,512]{0,1:T(8,128)(2,1)}, bf16[512,512]{0,1:T(8,128)(2,1)}), (bf16[512,512]{0,1:T(8,128)(2,1)}, bf16[512,512]{0,1:T(8,128)(2,1)}, ...) | async-done | bytes 2097168 | tf_op jit(solution)/shard_map/psum | solution.py:13
  303.0 4.0 reshape.191
  310.4 3.8 bitcast_select_fusion.6
  322.2 5.1 copy.58
  327.3 40.0 %all-reduce.13.cloned.1.call-done = bf16[512,512]{1,0:T(8,128)(2,1)} async-done(((bf16[512,512]{1,0:T(8,128)(2,1)}), bf16[512,512]{1,0:T(8,128)(2,1)}) %all-reduce.13.cloned.1.call-update) | async-done | bytes 524304 | tf_op jit(solution)/shard_map/psum | solution.py:58
  373.5 3.7 copy.59
  377.2 68.5 %all-gather.9.cloned.1.call-done = bf16[1,512,2048]{2,1,0:T(8,128)(2,1)} async-done(((bf16[1,16,2048]{2,1,0:T(8,128)(2,1)}), bf16[1,512,2048]{2,1,0:T(8,128)(2,1)}) %all-gather.9.cloned.1.call-update) | async-done | bytes 2097168 | tf_op jit(solution)/shard_map/all_gather | solution.py:39
  445.7 4.5 fusion.12
  450.2 51.0 %all-reduce.25 = bf16[512,512]{0,1:T(8,128)(2,1)S(1)} all-reduce(f32[512,512]{0,1:T(8,128)} %fusion.12), channel_id=1, replica_groups=mesh['row'=8,'col'=32] {'row'}, use_global_device_ids=true, to_apply=%region_18.19 | all-reduce | flops 262144 | bytes 1572864 | tf_op jit(solution)/shard_map/psum | solution.py:46
  503.4 152.1 %all-reduce.21.cloned.1.call-done = (bf16[512,512]{0,1:T(8,128)(2,1)}, bf16[512,512]{0,1:T(8,128)(2,1)}, bf16[512,512]{0,1:T(8,128)(2,1)}, bf16[512,512]{0,1:T(8,128)(2,1)}) async-done(((bf16[512,512]{0,1:T(8,128)(2,1)}, bf16[512,512]{0,1:T(8,128)(2,1)}, bf16[512,512]{0,1:T(8,128)(2,1)}, bf16[512,512]{0,1:T(8,128)(2,1)}), (bf16[512,512]{0,1:T(8,128)(2,1)}, bf16[512,512]{0,1:T(8,128)(2,1)}, ...) | async-done | bytes 2097168 | tf_op jit(solution)/shard_map/psum | solution.py:13
  664.7 4.4 copy.65
  669.1 5.2 bitcast_select_fusion.3
  674.3 4.1 reshape.223
  684.2 5.1 copy.70
  689.3 37.2 %all-reduce.15.cloned.1.call-done = bf16[512,512]{0,1:T(8,128)(2,1)} async-done(((bf16[512,512]{0,1:T(8,128)(2,1)}), bf16[512,512]{0,1:T(8,128)(2,1)}) %all-reduce.15.cloned.1.call-update) | async-done | bytes 524304 | tf_op jit(solution)/shard_map/psum | solution.py:58
  736.4 68.6 %all-gather.7.cloned.1.call-done = bf16[1,512,2048]{2,1,0:T(8,128)(2,1)} async-done(((bf16[1,16,2048]{2,1,0:T(8,128)(2,1)}), bf16[1,512,2048]{2,1,0:T(8,128)(2,1)}) %all-gather.7.cloned.1.call-update) | async-done | bytes 2097168 | tf_op jit(solution)/shard_map/all_gather | solution.py:39
  805.0 4.5 fusion.15
  809.5 50.8 %all-reduce.26 = bf16[512,512]{0,1:T(8,128)(2,1)S(1)} all-reduce(f32[512,512]{0,1:T(8,128)} %fusion.15), channel_id=1, replica_groups=mesh['row'=8,'col'=32] {'row'}, use_global_device_ids=true, to_apply=%region_24.25 | all-reduce | flops 262144 | bytes 1572864 | tf_op jit(solution)/shard_map/psum | solution.py:46
  865.1 149.7 %all-reduce.19.cloned.1.call-done = (bf16[512,512]{0,1:T(8,128)(2,1)}, bf16[512,512]{0,1:T(8,128)(2,1)}, bf16[512,512]{0,1:T(8,128)(2,1)}, bf16[512,512]{0,1:T(8,128)(2,1)}) async-done(((bf16[512,512]{0,1:T(8,128)(2,1)}, bf16[512,512]{0,1:T(8,128)(2,1)}, bf16[512,512]{0,1:T(8,128)(2,1)}, bf16[512,512]{0,1:T(8,128)(2,1)}), (bf16[512,512]{0,1:T(8,128)(2,1)}, bf16[512,512]{0,1:T(8,128)(2,1)}, ...) | async-done | bytes 2097168 | tf_op jit(solution)/shard_map/psum | solution.py:13
  1022.0 4.5 bitcast_select_fusion
  1034.6 4.2 copy.82
  1038.8 45.6 %all-reduce.17.cloned.1.call-done = bf16[512,512]{0,1:T(8,128)(2,1)} async-done(((bf16[512,512]{0,1:T(8,128)(2,1)}), bf16[512,512]{0,1:T(8,128)(2,1)}) %all-reduce.17.cloned.1.call-update) | async-done | bytes 524304 | tf_op jit(solution)/shard_map/psum | solution.py:58
  (114 shorter events, 87.7 us)
Async XLA Ops:
  6.5 83.0 %all-gather.11.cloned.1.call-start = ((), (), s32[]{:S(2)}) async-start(), calls=%async_computation.5 | async-start | bytes 2162688 | tf_op jit(solution)/shard_map/all_gather | solution.py:39
  8.1 289.5 %all-reduce.23.cloned.1.call-start = ((), (), s32[]{:S(2)}) async-start(), calls=%async_computation.8 | async-start | bytes 4194304 | tf_op jit(solution)/shard_map/psum | solution.py:13
  145.4 222.0 %all-reduce.13.cloned.1.call-start = ((), (), s32[]{:S(2)}) async-start(), calls=%async_computation | async-start | bytes 1048576 | tf_op jit(solution)/shard_map/psum | solution.py:58
  297.6 2.4 copy-start.6
  297.6 2.5 copy-start.4
  297.6 2.5 copy-start.9
  302.3 143.4 %all-gather.9.cloned.1.call-start = ((), (), s32[]{:S(2)}) async-start(), calls=%async_computation.4 | async-start | bytes 2162688 | tf_op jit(solution)/shard_map/all_gather | solution.py:39
  302.9 4.0 copy-start.8
  302.9 352.6 %all-reduce.21.cloned.1.call-start = ((), (), s32[]{:S(2)}) async-start(), calls=%async_computation.7 | async-start | bytes 4194304 | tf_op jit(solution)/shard_map/psum | solution.py:13
  503.4 223.2 %all-reduce.15.cloned.1.call-start = ((), (), s32[]{:S(2)}) async-start(), calls=%async_computation.1 | async-start | bytes 1048576 | tf_op jit(solution)/shard_map/psum | solution.py:58
  655.6 2.4 copy-start.7
  655.6 2.4 copy-start.5
  655.6 3.8 copy-start.10
  658.1 1.3 copy-start
  661.5 143.5 %all-gather.7.cloned.1.call-start = ((), (), s32[]{:S(2)}) async-start(), calls=%async_computation.3 | async-start | bytes 2162688 | tf_op jit(solution)/shard_map/all_gather | solution.py:39
  662.3 352.5 %all-reduce.19.cloned.1.call-start = ((), (), s32[]{:S(2)}) async-start(), calls=%async_computation.6 | async-start | bytes 4194304 | tf_op jit(solution)/shard_map/psum | solution.py:13
  664.7 4.4 copy-start.1
  862.6 221.9 %all-reduce.17.cloned.1.call-start = ((), (), s32[]{:S(2)}) async-start(), calls=%async_computation.2 | async-start | bytes 1048576 | tf_op jit(solution)/shard_map/psum | solution.py:58
  1014.8 2.4 copy-start.3
  1014.8 2.5 copy-start.2
  1014.8 2.5 copy-start.11
Sparse Core Ops, SparseCore 0:
  9.9 79.5 all-gather.10
  145.5 152.0 all-reduce.22
  302.4 64.8 all-reduce.12
  369.8 75.8 all-gather.8
  503.5 152.0 all-reduce.20
  661.6 64.8 all-reduce.14
  729.2 75.8 all-gather.6
  862.7 152.0 all-reduce.18
  1019.6 64.8 all-reduce.16
where the time goes:
time: 1100 us
  waiting for transfers between devices  795 us (72%)
  blocking collectives  152 us (14%)
  local copies, waits for them, and re-layouts  79 us (7%)
  matrix products  47 us (4%)
  between operations  13.6 us (1%)
  other arithmetic  13.1 us (1%)
    psum x3, waiting for transfers between devices, spread(): return lax.psum(kept, axis)  454 us
    all_gather x3, waiting for transfers between devices, local(): panel_rows = lax.all_gather(panels[supernode], 'col', axis=0, tiled=True)  217 us
    psum x3, blocking collectives, local(): col_sum = lax.psum(partial_value, 'row')  152 us
    psum x3, waiting for transfers between devices, local(): lax.psum(cross_part.astype(jnp.bfloat16), 'row').astype(jnp.float32)  123 us
  transfers between devices with their start and end apart: 9, of which 9 were waited for; matrix products, arithmetic and copies ran while one was open for 9% of the time, Pallas kernels for 0%

commit v1 on v0

--- a/solution.py
+++ b/solution.py
@@ -2,6 +2,7 @@
 import jax.numpy as jnp
 from jax import lax
 from jax.sharding import PartitionSpec as P
+from jax.lax import all_to_all, axis_size
 
 W = 512
 B = 128
@@ -36,7 +37,9 @@
         owned_blocks = supernode_blocks[supernode]
         row_flags = block_flags(listed, first_rowblock, row_blocks)
         col_flags = block_flags(listed, first_colblock, col_blocks)
-        panel_rows = lax.all_gather(panels[supernode], "col", axis=0, tiled=True)
+        panel_rows = jnp.concatenate(
+            all_to_all(jnp.stack([panels[supernode]] * axis_size("col")), "col", 0, 0), 0
+        )
         panel_rows = jnp.where(
             row_flags[None, :, None], panel_rows.reshape(W, row_blocks, B), 0
         ).reshape(W, local_rows)

time: 1100 us -> 995 us (0.905)
  waiting for transfers between devices: 795 us -> 639 us
  starting transfers between devices: 0.55 us -> 29.8 us
  other arithmetic: 13.1 us -> 25.7 us
    all_gather x3 -> x0, waiting for transfers between devices: 217 us -> none  [local(): panel_rows = lax.all_gather(panels[supernode], 'col', axis=0, tiled=True)]
    all_to_all x0 -> x3, waiting for transfers between devices: none -> 48.6 us  [local(): all_to_all(jnp.stack([panels[supernode]] * axis_size('col')), 'col', 0, 0)]
    all_to_all x0 -> x3, starting transfers between devices: none -> 28.7 us  [local(): all_to_all(jnp.stack([panels[supernode]] * axis_size('col')), 'col', 0, 0)]
    select_n x0 -> x5, other arithmetic: none -> 12.5 us  [local(): jnp.where(row_flags[None, :, None], panel_rows.reshape(W, row_blocks, B), 0)]
    psum x3, waiting for transfers between devices: 123 us -> 135 us  [local(): lax.psum(cross_part.astype(jnp.bfloat16), 'row').astype(jnp.float32)]
  transfers between devices with their start and end apart: 9 -> 9, of which waited for: 9 -> 7; matrix products, arithmetic and copies ran while one was open for 9% -> 11% of each run, Pallas kernels for 0% -> 0%
where the time goes in v1:
time: 995 us; the launch traced here: 989 us
  waiting for transfers between devices  639 us (64%)
  blocking collectives  156 us (16%)
  local copies, waits for them, and re-layouts  79.2 us (8%)
  matrix products  45.2 us (5%)
  starting transfers between devices  29.8 us (3%)
  other arithmetic  25.7 us (3%)
  between operations  14.2 us (1%)
    psum x3, waiting for transfers between devices, spread(): return lax.psum(kept, axis)  455 us
    psum x3, blocking collectives, local(): col_sum = lax.psum(partial_value, 'row')  156 us
    psum x3, waiting for transfers between devices, local(): lax.psum(cross_part.astype(jnp.bfloat16), 'row').astype(jnp.float32)  135 us
    all_to_all x3, waiting for transfers between devices, local(): all_to_all(jnp.stack([panels[supernode]] * axis_size('col')), 'col', 0, 0)  48.6 us
    all_to_all x3, starting transfers between devices, local(): all_to_all(jnp.stack([panels[supernode]] * axis_size('col')), 'col', 0, 0)  28.7 us
  transfers between devices with their start and end apart: 9, of which 7 were waited for; matrix products, arithmetic and copies ran while one was open for 11% of the time, Pallas kernels for 0%

profile of v1, /device:TPU:2, one launch (start us, length us, event | category | flops | bytes accessed | tf_op | source)
XLA Modules:
  0.0 989.4 jit_solution(12574699022169464330)
XLA Ops:
  9.0 11.7 %all-to-all-start.2 = ((bf16[32,16,2048]{2,1,0:T(8,128)(2,1)}), bf16[32,16,2048]{2,1,0:T(8,128)(2,1)S(1)}, u32[]{:S(2)}, u32[]{:S(2)}) async-start(bf16[32,16,2048]{2,1,0:T(8,128)(2,1)} %stack.11), calls=%async_computation.2 | async-start | bytes 4194304 | tf_op jit(solution)/shard_map/all_to_all | solution.py:41
  21.4 48.6 %all-to-all-done.2 = bf16[32,16,2048]{2,1,0:T(8,128)(2,1)S(1)} async-done(((bf16[32,16,2048]{2,1,0:T(8,128)(2,1)}), bf16[32,16,2048]{2,1,0:T(8,128)(2,1)S(1)}, u32[]{:S(2)}, u32[]{:S(2)}) %all-to-all-start.2) | async-done | bytes 2097184 | tf_op jit(solution)/shard_map/all_to_all | solution.py:41
  72.0 6.9 all-to-all-start.1
  84.4 52.9 %all-reduce.24 = bf16[512,512]{0,1:T(8,128)(2,1)S(1)} all-reduce(f32[512,512]{0,1:T(8,128)} %fusion.12), channel_id=1, replica_groups=mesh['row'=8,'col'=32] {'row'}, use_global_device_ids=true, to_apply=%region_12.13 | all-reduce | flops 262144 | bytes 1572864 | tf_op jit(solution)/shard_map/psum | solution.py:49
  139.6 4.0 reshape.206
  146.2 10.1 %all-to-all-start = ((bf16[32,16,2048]{2,1,0:T(8,128)(2,1)}), bf16[32,16,2048]{2,1,0:T(8,128)(2,1)}, u32[]{:S(2)}, u32[]{:S(2)}) async-start(bf16[32,16,2048]{2,1,0:T(8,128)(2,1)} %stack.9), calls=%async_computation | async-start | bytes 4194304 | tf_op jit(solution)/shard_map/all_to_all | solution.py:41
  157.9 160.8 %all-reduce.23.cloned.1.call-done = (bf16[512,512]{0,1:T(8,128)(2,1)}, bf16[512,512]{0,1:T(8,128)(2,1)}, bf16[512,512]{0,1:T(8,128)(2,1)}, bf16[512,512]{0,1:T(8,128)(2,1)}) async-done(((bf16[512,512]{0,1:T(8,128)(2,1)}, bf16[512,512]{0,1:T(8,128)(2,1)}, bf16[512,512]{0,1:T(8,128)(2,1)}, bf16[512,512]{0,1:T(8,128)(2,1)}), (bf16[512,512]{0,1:T(8,128)(2,1)}, bf16[512,512]{0,1:T(8,128)(2,1)}, ...) | async-done | bytes 2097168 | tf_op jit(solution)/shard_map/psum | solution.py:14
  326.5 3.8 bitcast_select_fusion.6
  338.3 5.1 copy.58
  343.4 45.0 %all-reduce.13.cloned.1.call-done = bf16[512,512]{1,0:T(8,128)(2,1)} async-done(((bf16[512,512]{1,0:T(8,128)(2,1)}), bf16[512,512]{1,0:T(8,128)(2,1)}) %all-reduce.13.cloned.1.call-update) | async-done | bytes 524304 | tf_op jit(solution)/shard_map/psum | solution.py:61
  394.6 3.7 copy.59
  398.3 4.5 fusion.6
  402.8 51.7 %all-reduce.25 = bf16[512,512]{0,1:T(8,128)(2,1)S(1)} all-reduce(f32[512,512]{0,1:T(8,128)} %fusion.6), channel_id=1, replica_groups=mesh['row'=8,'col'=32] {'row'}, use_global_device_ids=true, to_apply=%region_18.19 | all-reduce | flops 262144 | bytes 1572864 | tf_op jit(solution)/shard_map/psum | solution.py:49
  465.1 145.7 %all-reduce.21.cloned.1.call-done = (bf16[512,512]{0,1:T(8,128)(2,1)}, bf16[512,512]{0,1:T(8,128)(2,1)}, bf16[512,512]{0,1:T(8,128)(2,1)}, bf16[512,512]{0,1:T(8,128)(2,1)}) async-done(((bf16[512,512]{0,1:T(8,128)(2,1)}, bf16[512,512]{0,1:T(8,128)(2,1)}, bf16[512,512]{0,1:T(8,128)(2,1)}, bf16[512,512]{0,1:T(8,128)(2,1)}), (bf16[512,512]{0,1:T(8,128)(2,1)}, bf16[512,512]{0,1:T(8,128)(2,1)}, ...) | async-done | bytes 2097168 | tf_op jit(solution)/shard_map/psum | solution.py:14
  618.4 4.5 bitcast_select_fusion.3
  631.0 5.1 copy.70
  636.1 44.5 %all-reduce.15.cloned.1.call-done = bf16[512,512]{0,1:T(8,128)(2,1)} async-done(((bf16[512,512]{0,1:T(8,128)(2,1)}), bf16[512,512]{0,1:T(8,128)(2,1)}) %all-reduce.15.cloned.1.call-update) | async-done | bytes 524304 | tf_op jit(solution)/shard_map/psum | solution.py:61
  686.7 3.7 copy.71
  690.4 4.5 fusion.9
  694.9 51.7 %all-reduce.26 = bf16[512,512]{0,1:T(8,128)(2,1)S(1)} all-reduce(f32[512,512]{0,1:T(8,128)} %fusion.9), channel_id=1, replica_groups=mesh['row'=8,'col'=32] {'row'}, use_global_device_ids=true, to_apply=%region_24.25 | all-reduce | flops 262144 | bytes 1572864 | tf_op jit(solution)/shard_map/psum | solution.py:49
  754.3 148.6 %all-reduce.19.cloned.1.call-done = (bf16[512,512]{0,1:T(8,128)(2,1)}, bf16[512,512]{0,1:T(8,128)(2,1)}, bf16[512,512]{0,1:T(8,128)(2,1)}, bf16[512,512]{0,1:T(8,128)(2,1)}) async-done(((bf16[512,512]{0,1:T(8,128)(2,1)}, bf16[512,512]{0,1:T(8,128)(2,1)}, bf16[512,512]{0,1:T(8,128)(2,1)}, bf16[512,512]{0,1:T(8,128)(2,1)}), (bf16[512,512]{0,1:T(8,128)(2,1)}, bf16[512,512]{0,1:T(8,128)(2,1)}, ...) | async-done | bytes 2097168 | tf_op jit(solution)/shard_map/psum | solution.py:14
  910.2 4.5 bitcast_select_fusion
  922.8 4.2 copy.82
  927.0 45.6 %all-reduce.17.cloned.1.call-done = bf16[512,512]{0,1:T(8,128)(2,1)} async-done(((bf16[512,512]{0,1:T(8,128)(2,1)}), bf16[512,512]{0,1:T(8,128)(2,1)}) %all-reduce.17.cloned.1.call-update) | async-done | bytes 524304 | tf_op jit(solution)/shard_map/psum | solution.py:61
  (125 shorter events, 103.5 us)
Async XLA Ops:
  9.0 11.8 %copy-start.13 = (s32[3,64]{1,0:T(4,128)S(1)}, s32[3,64]{1,0:T(4,128)}, u32[]{:S(2)}) copy-start(s32[3,64]{1,0:T(4,128)} %param.9) | copy-start | bytes 2308
  9.0 61.0 %all-to-all-start.2 = ((bf16[32,16,2048]{2,1,0:T(8,128)(2,1)}), bf16[32,16,2048]{2,1,0:T(8,128)(2,1)S(1)}, u32[]{:S(2)}, u32[]{:S(2)}) async-start(bf16[32,16,2048]{2,1,0:T(8,128)(2,1)} %stack.11), calls=%async_computation.2 | async-start | bytes 4194304 | tf_op jit(solution)/shard_map/all_to_all | solution.py:41
  70.0 2.0 copy-start.1
  72.0 72.4 %all-to-all-start.1 = ((bf16[32,16,2048]{2,1,0:T(8,128)(2,1)}), bf16[32,16,2048]{2,1,0:T(8,128)(2,1)S(1)}, u32[]{:S(2)}, u32[]{:S(2)}) async-start(bf16[32,16,2048]{2,1,0:T(8,128)(2,1)} %stack.10), calls=%async_computation.1 | async-start | bytes 4194304 | tf_op jit(solution)/shard_map/all_to_all | solution.py:41
  78.9 239.8 %all-reduce.23.cloned.1.call-start = ((), (), s32[]{:S(2)}) async-start(), calls=%async_computation.8 | async-start | bytes 4194304 | tf_op jit(solution)/shard_map/psum | solution.py:14
  78.9 3.2 copy-start.2
  80.8 1.3 copy-start.3
  139.6 4.0 copy-start.14
  144.4 12.0 %copy-start = (bf16[32,16,2048]{2,1,0:T(8,128)(2,1)}, bf16[32,16,2048]{2,1,0:T(8,128)(2,1)S(1)}, u32[]{:S(2)}) copy-start(bf16[32,16,2048]{2,1,0:T(8,128)(2,1)S(1)} %all-to-all-done.1) | copy-start | bytes 6291460
  146.2 313.7 %all-to-all-start = ((bf16[32,16,2048]{2,1,0:T(8,128)(2,1)}), bf16[32,16,2048]{2,1,0:T(8,128)(2,1)}, u32[]{:S(2)}, u32[]{:S(2)}) async-start(bf16[32,16,2048]{2,1,0:T(8,128)(2,1)} %stack.9), calls=%async_computation | async-start | bytes 4194304 | tf_op jit(solution)/shard_map/all_to_all | solution.py:41
  156.3 232.1 %all-reduce.13.cloned.1.call-start = ((), (), s32[]{:S(2)}) async-start(), calls=%async_computation.3 | async-start | bytes 1048576 | tf_op jit(solution)/shard_map/psum | solution.py:61
  318.7 2.4 copy-start.8
  318.7 2.5 copy-start.7
  318.7 2.5 copy-start.4
  323.4 287.4 %all-reduce.21.cloned.1.call-start = ((), (), s32[]{:S(2)}) async-start(), calls=%async_computation.7 | async-start | bytes 4194304 | tf_op jit(solution)/shard_map/psum | solution.py:14
  456.7 223.9 %all-reduce.15.cloned.1.call-start = ((), (), s32[]{:S(2)}) async-start(), calls=%async_computation.4 | async-start | bytes 1048576 | tf_op jit(solution)/shard_map/psum | solution.py:61
  610.8 2.4 copy-start.10
  610.8 2.5 copy-start.9
  610.8 2.5 copy-start.5
  615.6 287.3 %all-reduce.19.cloned.1.call-start = ((), (), s32[]{:S(2)}) async-start(), calls=%async_computation.6 | async-start | bytes 4194304 | tf_op jit(solution)/shard_map/psum | solution.py:14
  748.7 223.9 %all-reduce.17.cloned.1.call-start = ((), (), s32[]{:S(2)}) async-start(), calls=%async_computation.5 | async-start | bytes 1048576 | tf_op jit(solution)/shard_map/psum | solution.py:61
  902.9 2.4 copy-start.12
  902.9 2.5 copy-start.11
  902.9 2.5 copy-start.6
Sparse Core Ops, SparseCore 0:
  139.7 178.9 all-reduce.22
  323.5 64.8 all-reduce.12
  456.8 154.0 all-reduce.20
  615.7 64.8 all-reduce.14
  748.9 154.0 all-reduce.18
  907.8 64.7 all-reduce.16
